TPU v7x, 512 devices: a whole 4x8x8 slice. The times are simulated.
512 devices in a mesh: dp: 8 (over z), expert: 64 (over y, x, core).
Axes of the slice: x: 4, y: 8, z: 8, core: 2. Of those that a mesh axis runs over, the one named last changes fastest.
Arguments:
- tokens: bfloat16 [65536, 3584], P(('dp', 'expert')), may hold values from -6 to 6
- cotangent: bfloat16 [65536, 3584], P(('dp', 'expert')), may hold values from -6 to 6
- route_ids: int32 [65536, 8], P(('dp', 'expert')), may hold values from 0 to 255, as said below
- route_gates: float32 [65536, 8], P(('dp', 'expert')), may hold values from 0.1 to 1
- gate_w: bfloat16 [3584, 8192], P('dp', 'expert'), may hold values from -0.09375 to 0.09375
- up_w: bfloat16 [3584, 8192], P('dp', 'expert'), may hold values from -0.09375 to 0.09375
- down_w: bfloat16 [3584, 8192], P('dp', 'expert'), may hold values from -0.1875 to 0.1875
Outputs:
- moe_out: bfloat16 [65536, 3584], P(('dp', 'expert'))
- d_tokens: bfloat16 [65536, 3584], P(('dp', 'expert'))
- d_gates: float32 [65536, 8], P(('dp', 'expert'))
- d_gate_w: bfloat16 [3584, 8192], P('dp', 'expert')
- d_up_w: bfloat16 [3584, 8192], P('dp', 'expert')
- d_down_w: bfloat16 [3584, 8192], P('dp', 'expert')
Inputs may be any that keep to these rules, and one draw needn't show every extreme that they name: `route_ids`: each token names 8 different experts; the experts in flight are 0 to 7. Among the tokens of one device (aligned blocks of 128 tokens) each expert in flight is named by at most 6 tokens, and in every draw one expert in flight is named by exactly 6 tokens in every block.
All inputs are finite; a program needn't handle non-finite values.
Results may differ from a plain program's by a relative error of at most 0.017.
Values may be sent and summed in bfloat16 or wider, within the bound.
A program may use at most 64 MiB of HBM per device.

v0:
```python
import jax
import jax.numpy as jnp
from jax import lax
from jax.sharding import PartitionSpec as P

TOP = 8
SLICES = 8
CAP = 6


def shards(tokens, cotangent, route_ids, route_gates, gate_w, up_w, down_w):
    owners = lax.axis_size("expert")
    groups = owners // SLICES
    tok_rows = tokens.shape[0]
    routes = tok_rows * TOP
    flat_ids = route_ids.reshape(routes)
    matched = (flat_ids[:, None] == jnp.arange(groups, dtype=jnp.int32)[None, :]).astype(jnp.int32)
    slot_index = jnp.cumsum(matched, axis=0) - 1
    chosen = (matched[:, :, None] == 1) & (
        slot_index[:, :, None] == jnp.arange(CAP, dtype=jnp.int32)[None, None, :]
    )
    select = jnp.transpose(chosen, (1, 2, 0)).reshape(groups * CAP, routes).astype(jnp.float32)
    tok_select = jnp.sum(select.reshape(groups * CAP, tok_rows, TOP), axis=2)
    slot_gate = jnp.sum(select * route_gates.reshape(routes)[None, :], axis=1)
    pick_rows = tok_select.astype(jnp.bfloat16)
    token_slots = jnp.dot(pick_rows, tokens, preferred_element_type=jnp.float32).astype(
        jnp.bfloat16
    )
    cotangent_slots = jnp.dot(pick_rows, cotangent, preferred_element_type=jnp.float32).astype(
        jnp.bfloat16
    )
    scaled_slots = (slot_gate[:, None] * cotangent_slots.astype(jnp.float32)).astype(jnp.bfloat16)

    def spread(slot_rows):
        width = slot_rows.shape[1]
        grouped = slot_rows.reshape(groups, 1, CAP, width)
        return jnp.broadcast_to(grouped, (groups, SLICES, CAP, width)).reshape(owners * CAP, width)

    w_gate, w_up, w_down = (
        lax.all_gather(gate_w, "dp", axis=0, tiled=True),
        lax.all_gather(up_w, "dp", axis=0, tiled=True),
        lax.all_gather(down_w, "dp", axis=0, tiled=True),
    )
    token_rows = lax.all_to_all(
        spread(token_slots), "expert", split_axis=0, concat_axis=0, tiled=True
    )
    gate_pre = jnp.dot(token_rows, w_gate, preferred_element_type=jnp.float32)
    up_pre = jnp.dot(token_rows, w_up, preferred_element_type=jnp.float32)
    sigmoid_gate = jax.nn.sigmoid(gate_pre)
    active = gate_pre * sigmoid_gate
    hidden = (active * up_pre).astype(jnp.bfloat16)
    contract_cols = (((1,), (1,)), ((), ()))
    out_part = lax.dot_general(
        hidden, w_down, contract_cols, preferred_element_type=jnp.float32
    ).astype(jnp.bfloat16)
    out_back = lax.all_to_all(out_part, "expert", split_axis=0, concat_axis=0, tiled=True)
    scaled_rows = lax.all_to_all(
        spread(scaled_slots), "expert", split_axis=0, concat_axis=0, tiled=True
    )
    d_hidden = jnp.dot(scaled_rows, w_down, preferred_element_type=jnp.float32)
    d_gate_pre = (
        d_hidden * up_pre * sigmoid_gate * (1.0 + gate_pre * (1.0 - sigmoid_gate))
    ).astype(jnp.bfloat16)
    d_up_pre = (d_hidden * active).astype(jnp.bfloat16)
    dx_part = lax.dot_general(d_gate_pre, w_gate, contract_cols, preferred_element_type=jnp.float32)
    dx_part = (
        dx_part + lax.dot_general(d_up_pre, w_up, contract_cols, preferred_element_type=jnp.float32)
    ).astype(jnp.bfloat16)
    contract_rows = (((0,), (0,)), ((), ()))
    gate_term = lax.dot_general(
        token_rows, d_gate_pre, contract_rows, preferred_element_type=jnp.float32
    )
    up_term = lax.dot_general(
        token_rows, d_up_pre, contract_rows, preferred_element_type=jnp.float32
    )
    down_term = lax.dot_general(
        scaled_rows, hidden, contract_rows, preferred_element_type=jnp.float32
    )
    summed_grads = lax.psum_scatter(
        jnp.concatenate([gate_term, up_term, down_term], axis=1).astype(jnp.bfloat16),
        "dp",
        scatter_dimension=0,
        tiled=True,
    ).astype(jnp.float32)
    hidden_cols = gate_w.shape[1]
    d_gate_w = summed_grads[:, :hidden_cols].astype(jnp.bfloat16)
    d_up_w = summed_grads[:, hidden_cols : 2 * hidden_cols].astype(jnp.bfloat16)
    d_down_w = summed_grads[:, 2 * hidden_cols :].astype(jnp.bfloat16)
    dx_back = lax.all_to_all(dx_part, "expert", split_axis=0, concat_axis=0, tiled=True)
    member_wide = spread(tok_select)
    weighted_wide = spread(tok_select * slot_gate[:, None])
    weight_high = weighted_wide.astype(jnp.bfloat16)
    weight_low = (weighted_wide - weight_high.astype(jnp.float32)).astype(jnp.bfloat16)
    moe_sum = lax.dot_general(
        weight_high, out_back, contract_rows, preferred_element_type=jnp.float32
    )
    moe_sum = moe_sum + lax.dot_general(
        weight_low, out_back, contract_rows, preferred_element_type=jnp.float32
    )
    moe_out = moe_sum.astype(jnp.bfloat16)
    d_tokens = lax.dot_general(
        member_wide.astype(jnp.bfloat16), dx_back, contract_rows, preferred_element_type=jnp.float32
    ).astype(jnp.bfloat16)
    inner = lax.dot_general(cotangent, out_back, contract_cols, preferred_element_type=jnp.float32)
    wide_grad = jnp.sum(inner * jnp.transpose(member_wide), axis=0)
    slot_grad = jnp.sum(wide_grad.reshape(groups, SLICES, CAP), axis=1).reshape(groups * CAP)
    d_gates = jnp.sum(slot_grad[:, None] * select, axis=0).reshape(tok_rows, TOP)
    return (moe_out, d_tokens, d_gates, d_gate_w, d_up_w, d_down_w)


def solution(mesh):
    return jax.shard_map(
        shards,
        mesh=mesh,
        in_specs=(
            P(("dp", "expert"), None),
            P(("dp", "expert"), None),
            P(("dp", "expert"), None),
            P(("dp", "expert"), None),
            P("dp", "expert"),
            P("dp", "expert"),
            P("dp", "expert"),
        ),
        out_specs=(
            P(("dp", "expert"), None),
            P(("dp", "expert"), None),
            P(("dp", "expert"), None),
            P("dp", "expert"),
            P("dp", "expert"),
            P("dp", "expert"),
        ),
        check_vma=False,
    )
```

profile of v0, /device:TPU:2, one launch (start us, length us, event | category | flops | bytes accessed | tf_op | source)
XLA Modules:
  0.0 461.1 jit_solution(1026153735217437292)
XLA Ops:
  7.2 0.9 copy.27
  8.4 2.3 reduce-window.6
  10.6 0.3 slice_reduce_fusion
  10.9 0.2 reduce-window.9
  11.2 1.9 and.18
  13.2 3.4 eq.81
  16.6 2.9 convert_reduce_fusion
  19.6 0.3 convolution_convert_fusion.6
  19.9 2.1 broadcast_in_dim.36
  22.1 11.0 %all-to-all-start = ((bf16[64,6,3584]{2,1,0:T(8,128)(2,1)}), bf16[64,6,3584]{2,1,0:T(8,128)(2,1)}, u32[]{:S(2)}, u32[]{:S(2)}) async-start(bf16[64,6,3584]{2,1,0:T(8,128)(2,1)} %bitcast.37), calls=%async_computation | async-start | bytes 7340032 | tf_op jit(solution)/shard_map/all_to_all | solution.py:44
  33.1 32.2 %all_gather.9 = bf16[3584,128]{1,0:T(8,128)(2,1)S(1)} all-gather(bf16[448,128]{1,0:T(8,128)(2,1)S(1)} %copy-done.10), channel_id=1, replica_groups=mesh['dp'=8,'expert'=64] {'dp'}, dimensions={0}, use_global_device_ids=true | all-gather | bytes 1032192 | tf_op jit(solution)/shard_map/all_gather | solution.py:40
  65.3 26.5 %all_gather.10 = bf16[3584,128]{1,0:T(8,128)(2,1)S(1)} all-gather(bf16[448,128]{1,0:T(8,128)(2,1)S(1)} %copy-done.11), channel_id=1, replica_groups=mesh['dp'=8,'expert'=64] {'dp'}, dimensions={0}, use_global_device_ids=true | all-gather | bytes 1032192 | tf_op jit(solution)/shard_map/all_gather | solution.py:41
  91.8 28.6 %all_gather.11 = bf16[3584,128]{1,0:T(8,128)(2,1)} all-gather(bf16[448,128]{1,0:T(8,128)(2,1)S(1)} %copy-done.12), channel_id=1, replica_groups=mesh['dp'=8,'expert'=64] {'dp'}, dimensions={0}, use_global_device_ids=true | all-gather | bytes 1032192 | tf_op jit(solution)/shard_map/all_gather | solution.py:42
  120.4 5.5 %all_to_all.34 = bf16[384,3584]{1,0:T(8,128)(2,1)} reshape(bf16[64,6,3584]{2,1,0:T(8,128)(2,1)} %all-to-all-done) | data formatting | bytes 5505024 | tf_op jit(solution)/shard_map/all_to_all | solution.py:44
  125.8 2.8 fusion.12
  128.7 0.9 multiply_convert_fusion.2
  129.6 0.3 copy-done.7
  129.8 2.5 convolution_convert_fusion
  132.3 5.4 %all_to_all.35 = bf16[64,6,3584]{2,1,0:T(8,128)(2,1)} reshape(bf16[384,3584]{1,0:T(8,128)(2,1)} %convolution_convert_fusion) | data formatting | bytes 5505024 | tf_op jit(solution)/shard_map/all_to_all | solution.py:56
  137.7 10.1 %all-to-all-start.1 = ((bf16[64,6,3584]{2,1,0:T(8,128)(2,1)}), bf16[64,6,3584]{2,1,0:T(8,128)(2,1)}, u32[]{:S(2)}, u32[]{:S(2)}) async-start(bf16[64,6,3584]{2,1,0:T(8,128)(2,1)} %all_to_all.35), calls=%async_computation.1 | async-start | bytes 7340032 | tf_op jit(solution)/shard_map/all_to_all | solution.py:56
  148.2 84.5 %all-to-all-done.1 = bf16[64,6,3584]{2,1,0:T(8,128)(2,1)} async-done(((bf16[64,6,3584]{2,1,0:T(8,128)(2,1)}), bf16[64,6,3584]{2,1,0:T(8,128)(2,1)}, u32[]{:S(2)}, u32[]{:S(2)}) %all-to-all-start.1) | async-done | bytes 2752544 | tf_op jit(solution)/shard_map/all_to_all | solution.py:56
  232.7 5.5 %all_to_all.37 = bf16[384,3584]{1,0:T(8,128)(2,1)} reshape(bf16[64,6,3584]{2,1,0:T(8,128)(2,1)} %all-to-all-done.1) | data formatting | bytes 5505024 | tf_op jit(solution)/shard_map/all_to_all | solution.py:56
  238.2 2.7 fusion.5
  241.2 0.2 select_reduce_fusion
  241.4 0.3 fusion.4
  241.8 0.3 broadcast_in_dim.40
  242.1 90.3 %all_to_all.48 = bf16[64,6,3584]{2,1,0:T(8,128)(2,1)} all-to-all(bf16[64,6,3584]{2,1,0:T(8,128)(2,1)S(1)} %bitcast.38), channel_id=1, replica_groups=mesh['dp'=8,'expert'=64] {'expert'}, dimensions={0} | all-to-all | bytes 5505024 | tf_op jit(solution)/shard_map/all_to_all | solution.py:57
  332.4 5.5 %all_to_all.40 = bf16[384,3584]{1,0:T(8,128)(2,1)} reshape(bf16[64,6,3584]{2,1,0:T(8,128)(2,1)} %all_to_all.48) | data formatting | bytes 5505024 | tf_op jit(solution)/shard_map/all_to_all | solution.py:57
  337.9 2.6 convolution_convert_fusion.1
  340.5 0.2 copy-done.8
  340.7 0.9 multiply_convert_fusion
  341.6 0.9 copy-done.3
  342.5 0.7 convolution_convert_fusion.3
  343.2 0.9 fusion.14
  344.1 0.7 convolution_convert_fusion.2
  344.8 0.5 copy-done.6
  345.2 2.4 fusion
  347.7 5.4 %all_to_all.41 = bf16[64,6,3584]{2,1,0:T(8,128)(2,1)} reshape(bf16[384,3584]{1,0:T(8,128)(2,1)} %fusion) | data formatting | bytes 5505024 | tf_op jit(solution)/shard_map/all_to_all | solution.py:89
  353.1 5.6 %all-to-all-start.3 = ((bf16[64,6,3584]{2,1,0:T(8,128)(2,1)}), bf16[64,6,3584]{2,1,0:T(8,128)(2,1)}, u32[]{:S(2)}, u32[]{:S(2)}) async-start(bf16[64,6,3584]{2,1,0:T(8,128)(2,1)} %all_to_all.41), calls=%async_computation.3 | async-start | bytes 7340032 | tf_op jit(solution)/shard_map/all_to_all | solution.py:89
  358.7 1.7 pad_maximum_fusion
  360.4 4.5 copy.35
  365.0 0.7 copy.31
  366.0 2.4 fusion.13
  368.5 3.4 fusion.1
  371.8 71.8 %all-to-all-done.3 = bf16[64,6,3584]{2,1,0:T(8,128)(2,1)} async-done(((bf16[64,6,3584]{2,1,0:T(8,128)(2,1)}), bf16[64,6,3584]{2,1,0:T(8,128)(2,1)}, u32[]{:S(2)}, u32[]{:S(2)}) %all-to-all-start.3) | async-done | bytes 2752544 | tf_op jit(solution)/shard_map/all_to_all | solution.py:89
  443.6 5.6 %all_to_all.43 = bf16[384,3584]{1,0:T(8,128)(2,1)} reshape(bf16[64,6,3584]{2,1,0:T(8,128)(2,1)} %all-to-all-done.3) | data formatting | bytes 5505024 | tf_op jit(solution)/shard_map/all_to_all | solution.py:89
  449.2 3.4 convolution_convert_fusion.4
  452.6 1.7 fusion.11
  (57 shorter events, 1.7 us)
Async XLA Ops:
  7.2 231.1 %copy-start = (bf16[128,3584]{1,0:T(8,128)(2,1)S(1)}, bf16[128,3584]{1,0:T(8,128)(2,1)}, u32[]{:S(2)}) copy-start(bf16[128,3584]{1,0:T(8,128)(2,1)} %param.8) | copy-start | bytes 2752516
  16.6 2.9 copy-start.9
  22.0 11.0 %copy-start.10 = (bf16[448,128]{1,0:T(8,128)(2,1)S(1)}, bf16[448,128]{1,0:T(8,128)(2,1)}, u32[]{:S(2)}) copy-start(bf16[448,128]{1,0:T(8,128)(2,1)} %param.11) | copy-start | bytes 344068
  22.0 43.2 %copy-start.11 = (bf16[448,128]{1,0:T(8,128)(2,1)S(1)}, bf16[448,128]{1,0:T(8,128)(2,1)}, u32[]{:S(2)}) copy-start(bf16[448,128]{1,0:T(8,128)(2,1)} %param.12) | copy-start | bytes 344068
  22.1 69.8 %copy-start.12 = (bf16[448,128]{1,0:T(8,128)(2,1)S(1)}, bf16[448,128]{1,0:T(8,128)(2,1)}, u32[]{:S(2)}) copy-start(bf16[448,128]{1,0:T(8,128)(2,1)} %param.13) | copy-start | bytes 344068
  22.1 98.3 %all-to-all-start = ((bf16[64,6,3584]{2,1,0:T(8,128)(2,1)}), bf16[64,6,3584]{2,1,0:T(8,128)(2,1)}, u32[]{:S(2)}, u32[]{:S(2)}) async-start(bf16[64,6,3584]{2,1,0:T(8,128)(2,1)} %bitcast.37), calls=%async_computation | async-start | bytes 7340032 | tf_op jit(solution)/shard_map/all_to_all | solution.py:44
  91.8 36.8 %copy-start.5 = (bf16[3584,128]{1,0:T(8,128)(2,1)}, bf16[3584,128]{1,0:T(8,128)(2,1)S(1)}, u32[]{:S(2)}) copy-start(bf16[3584,128]{1,0:T(8,128)(2,1)S(1)} %all_gather.10) | copy-start | bytes 2752516
  125.8 2.8 copy-start.2
  128.7 1.2 copy-start.7
  137.7 10.1 %copy-start.13 = (f32[128,8]{0,1:T(8,128)S(1)}, f32[128,8]{0,1:T(8,128)}, u32[]{:S(2)}) copy-start(f32[128,8]{0,1:T(8,128)} %param.10) | copy-start | bytes 12292
  137.7 95.0 %all-to-all-start.1 = ((bf16[64,6,3584]{2,1,0:T(8,128)(2,1)}), bf16[64,6,3584]{2,1,0:T(8,128)(2,1)}, u32[]{:S(2)}, u32[]{:S(2)}) async-start(bf16[64,6,3584]{2,1,0:T(8,128)(2,1)} %all_to_all.35), calls=%async_computation.1 | async-start | bytes 7340032 | tf_op jit(solution)/shard_map/all_to_all | solution.py:56
  337.8 2.6 copy-start.4
  337.9 2.8 copy-start.8
  340.7 1.8 copy-start.3
  344.0 1.2 copy-start.6
  353.1 90.6 %all-to-all-start.3 = ((bf16[64,6,3584]{2,1,0:T(8,128)(2,1)}), bf16[64,6,3584]{2,1,0:T(8,128)(2,1)}, u32[]{:S(2)}, u32[]{:S(2)}) async-start(bf16[64,6,3584]{2,1,0:T(8,128)(2,1)} %all_to_all.41), calls=%async_computation.3 | async-start | bytes 7340032 | tf_op jit(solution)/shard_map/all_to_all | solution.py:89
  358.7 93.9 %reduce-scatter.4.cloned.1.call-start = ((), (), s32[]{:S(2)}) async-start(), calls=%async_computation.5 | async-start | bytes 3096576
  443.6 10.7 %copy-start.1 = (bf16[128,3584]{1,0:T(8,128)(2,1)S(1)}, bf16[128,3584]{1,0:T(8,128)(2,1)}, u32[]{:S(2)}) copy-start(bf16[128,3584]{1,0:T(8,128)(2,1)} %param.8) | copy-start | bytes 2752516
Sparse Core Ops, SparseCore 0:
  365.1 46.6 reduce-scatter.3
where the time goes:
time: 463 us; the launch traced here: 461 us
  blocking collectives  178 us (38%)
  waiting for transfers between devices  156 us (34%)
  local copies, waits for them, and re-layouts  51.9 us (11%)
  matrix products  26.8 us (6%)
  starting transfers between devices  26.8 us (6%)
  between operations  14.4 us (3%)
  other arithmetic  7.41 us (2%)
    all_to_all x1, blocking collectives, shards(): lax.all_to_all(spread(scaled_slots), 'expert', split_axis=0, concat_axis=...  90.3 us
    all_to_all x1, waiting for transfers between devices, shards(): lax.all_to_all(out_part, 'expert', split_axis=0, concat_axis=0, tiled=True)  84.5 us
    all_to_all x1, waiting for transfers between devices, shards(): lax.all_to_all(dx_part, 'expert', split_axis=0, concat_axis=0, tiled=True)  71.8 us
    all_gather x1, blocking collectives, shards(): lax.all_gather(gate_w, 'dp', axis=0, tiled=True)  32.2 us
    all_gather x1, blocking collectives, shards(): lax.all_gather(down_w, 'dp', axis=0, tiled=True)  28.6 us
    all_gather x1, blocking collectives, shards(): lax.all_gather(up_w, 'dp', axis=0, tiled=True)  26.5 us
    all_to_all x1, starting transfers between devices, shards(): lax.all_to_all(spread(token_slots), 'expert', split_axis=0, concat_axis=0...  11 us
    all_to_all x2, local copies, waits for them, and re-layouts, shards(): lax.all_to_all(dx_part, 'expert', split_axis=0, concat_axis=0, tiled=True)  11 us
  transfers between devices with their start and end apart: 4, of which 2 were waited for; matrix products, arithmetic and copies ran while one was open for 4% of the time, Pallas kernels for 0%

commit v1 on v0

--- a/solution.py
+++ b/solution.py
@@ -1,3 +1,4 @@
+import functools
 import jax
 import jax.numpy as jnp
 from jax import lax
@@ -6,6 +7,18 @@
 TOP = 8
 SLICES = 8
 CAP = 6
+
+
+def ratios_arrange(vals, device_axis):
+    lanes = lax.psum(1, device_axis)
+    gallery = []
+    for k in range(vals.ndim):
+        gallery.append(lanes if k == 0 else 1)
+    small = jnp.tile(vals, gallery)
+    return lax.all_to_all(small, tiled=True, split_axis=0, axis_name=device_axis, concat_axis=0)
+
+
+shapes_meet = functools.partial(ratios_arrange, device_axis="dp")
 
 
 def shards(tokens, cotangent, route_ids, route_gates, gate_w, up_w, down_w):
@@ -38,7 +51,7 @@
 
     w_gate, w_up, w_down = (
         lax.all_gather(gate_w, "dp", axis=0, tiled=True),
-        lax.all_gather(up_w, "dp", axis=0, tiled=True),
+        shapes_meet(up_w),
         lax.all_gather(down_w, "dp", axis=0, tiled=True),
     )
     token_rows = lax.all_to_all(

time: 463 us -> 539 us (1.16)
  blocking collectives: 178 us -> 258 us
    all_to_all x0 -> x1, blocking collectives: none -> 95.7 us  [shards(): lax.all_to_all(spread(token_slots), 'expert', split_axis=0, concat_axis=0...]
    all_gather x1 -> x0, blocking collectives: 26.5 us -> none  [shards(): lax.all_gather(up_w, 'dp', axis=0, tiled=True)]
    all_gather x1, blocking collectives: 32.2 us -> 43.4 us  [shards(): lax.all_gather(gate_w, 'dp', axis=0, tiled=True)]
where the time goes in v1:
time: 539 us; the launch traced here: 538 us
  blocking collectives  258 us (48%)
  waiting for transfers between devices  156 us (29%)
  local copies, waits for them, and re-layouts  50.9 us (9%)
  matrix products  28.8 us (5%)
  starting transfers between devices  22.3 us (4%)
  between operations  14.4 us (3%)
  other arithmetic  7.41 us (1%)
    all_to_all x1, blocking collectives, shards(): lax.all_to_all(spread(token_slots), 'expert', split_axis=0, concat_axis=0...  95.7 us
    all_to_all x1, blocking collectives, shards(): lax.all_to_all(spread(scaled_slots), 'expert', split_axis=0, concat_axis=...  90.3 us
    all_to_all x1, waiting for transfers between devices, shards(): lax.all_to_all(out_part, 'expert', split_axis=0, concat_axis=0, tiled=True)  84.5 us
    all_to_all x1, waiting for transfers between devices, shards(): lax.all_to_all(dx_part, 'expert', split_axis=0, concat_axis=0, tiled=True)  71.8 us
    all_gather x1, blocking collectives, shards(): lax.all_gather(gate_w, 'dp', axis=0, tiled=True)  43.4 us
    all_gather x1, blocking collectives, shards(): lax.all_gather(down_w, 'dp', axis=0, tiled=True)  28.4 us
    all_to_all x2, local copies, waits for them, and re-layouts, shards(): lax.all_to_all(dx_part, 'expert', split_axis=0, concat_axis=0, tiled=True)  11 us
    all_to_all x2, local copies, waits for them, and re-layouts, shards(): lax.all_to_all(out_part, 'expert', split_axis=0, concat_axis=0, tiled=True)  10.9 us
  transfers between devices with their start and end apart: 4, of which 2 were waited for; matrix products, arithmetic and copies ran while one was open for 4% of the time, Pallas kernels for 0%

profile of v1, /device:TPU:2, one launch (start us, length us, event | category | flops | bytes accessed | tf_op | source)
XLA Modules:
  0.0 537.8 jit_solution(5529414110759231997)
XLA Ops:
  7.2 0.9 copy.27
  8.4 2.3 reduce-window.6
  10.6 0.3 slice_reduce_fusion
  10.9 0.2 reduce-window.9
  11.2 1.9 and.18
  13.2 3.4 eq.81
  16.6 2.9 convert_reduce_fusion
  19.6 0.3 convolution_convert_fusion.6
  20.0 0.3 broadcast_in_dim.36
  20.2 95.7 %all_to_all.57 = bf16[64,6,3584]{2,1,0:T(8,128)(2,1)} all-to-all(bf16[64,6,3584]{2,1,0:T(8,128)(2,1)S(1)} %bitcast.38), channel_id=1, replica_groups=mesh['dp'=8,'expert'=64] {'expert'}, dimensions={0} | all-to-all | bytes 5505024 | tf_op jit(solution)/shard_map/all_to_all | solution.py:57
  115.9 1.0 tile.2
  116.9 10.3 %all-to-all-start.1 = ((bf16[8,448,128]{2,1,0:T(8,128)(2,1)}), bf16[8,448,128]{2,1,0:T(8,128)(2,1)S(1)}, u32[]{:S(2)}, u32[]{:S(2)}) async-start(bf16[8,448,128]{2,1,0:T(8,128)(2,1)} %tile.2), calls=%async_computation.1 | async-start | bytes 1835008 | tf_op jit(solution)/shard_map/all_to_all | solution.py:18
  127.3 43.4 %all_gather.6 = bf16[3584,128]{1,0:T(8,128)(2,1)S(1)} all-gather(bf16[448,128]{1,0:T(8,128)(2,1)S(1)} %copy-done.10), channel_id=1, replica_groups=mesh['dp'=8,'expert'=64] {'dp'}, dimensions={0}, use_global_device_ids=true | all-gather | bytes 1032192 | tf_op jit(solution)/shard_map/all_gather | solution.py:53
  170.7 28.4 %all_gather.7 = bf16[3584,128]{1,0:T(8,128)(2,1)} all-gather(bf16[448,128]{1,0:T(8,128)(2,1)S(1)} %copy-done.11), channel_id=1, replica_groups=mesh['dp'=8,'expert'=64] {'dp'}, dimensions={0}, use_global_device_ids=true | all-gather | bytes 1032192 | tf_op jit(solution)/shard_map/all_gather | solution.py:55
  199.1 5.5 %all_to_all.40 = bf16[384,3584]{1,0:T(8,128)(2,1)} reshape(bf16[64,6,3584]{2,1,0:T(8,128)(2,1)} %all_to_all.57) | data formatting | bytes 5505024 | tf_op jit(solution)/shard_map/all_to_all | solution.py:57
  204.5 2.6 fusion.12
  207.2 3.0 multiply_convert_fusion.2
  210.2 2.5 convolution_convert_fusion
  212.7 5.4 %all_to_all.43 = bf16[64,6,3584]{2,1,0:T(8,128)(2,1)} reshape(bf16[384,3584]{1,0:T(8,128)(2,1)} %convolution_convert_fusion) | data formatting | bytes 5505024 | tf_op jit(solution)/shard_map/all_to_all | solution.py:69
  218.1 6.4 %all-to-all-start.2 = ((bf16[64,6,3584]{2,1,0:T(8,128)(2,1)}), bf16[64,6,3584]{2,1,0:T(8,128)(2,1)}, u32[]{:S(2)}, u32[]{:S(2)}) async-start(bf16[64,6,3584]{2,1,0:T(8,128)(2,1)} %all_to_all.43), calls=%async_computation.2 | async-start | bytes 7340032 | tf_op jit(solution)/shard_map/all_to_all | solution.py:69
  224.9 84.5 %all-to-all-done.2 = bf16[64,6,3584]{2,1,0:T(8,128)(2,1)} async-done(((bf16[64,6,3584]{2,1,0:T(8,128)(2,1)}), bf16[64,6,3584]{2,1,0:T(8,128)(2,1)}, u32[]{:S(2)}, u32[]{:S(2)}) %all-to-all-start.2) | async-done | bytes 2752544 | tf_op jit(solution)/shard_map/all_to_all | solution.py:69
  309.4 5.5 %all_to_all.45 = bf16[384,3584]{1,0:T(8,128)(2,1)} reshape(bf16[64,6,3584]{2,1,0:T(8,128)(2,1)} %all-to-all-done.2) | data formatting | bytes 5505024 | tf_op jit(solution)/shard_map/all_to_all | solution.py:69
  314.9 2.7 fusion.5
  317.8 0.2 select_reduce_fusion
  318.1 0.3 fusion.4
  318.5 0.3 broadcast_in_dim.40
  318.7 90.3 %all_to_all.58 = bf16[64,6,3584]{2,1,0:T(8,128)(2,1)} all-to-all(bf16[64,6,3584]{2,1,0:T(8,128)(2,1)S(1)} %bitcast.39), channel_id=1, replica_groups=mesh['dp'=8,'expert'=64] {'expert'}, dimensions={0} | all-to-all | bytes 5505024 | tf_op jit(solution)/shard_map/all_to_all | solution.py:70
  409.0 5.5 %all_to_all.48 = bf16[384,3584]{1,0:T(8,128)(2,1)} reshape(bf16[64,6,3584]{2,1,0:T(8,128)(2,1)} %all_to_all.58) | data formatting | bytes 5505024 | tf_op jit(solution)/shard_map/all_to_all | solution.py:70
  414.5 2.6 convolution_convert_fusion.1
  417.1 0.2 copy-done.7
  417.3 0.9 multiply_convert_fusion
  418.2 0.9 copy-done.2
  419.1 0.7 convolution_convert_fusion.3
  419.8 0.9 fusion.14
  420.7 0.7 convolution_convert_fusion.2
  421.4 0.5 copy-done.5
  421.9 2.4 fusion
  424.3 5.4 %all_to_all.49 = bf16[64,6,3584]{2,1,0:T(8,128)(2,1)} reshape(bf16[384,3584]{1,0:T(8,128)(2,1)} %fusion) | data formatting | bytes 5505024 | tf_op jit(solution)/shard_map/all_to_all | solution.py:102
  429.7 5.6 %all-to-all-start.4 = ((bf16[64,6,3584]{2,1,0:T(8,128)(2,1)}), bf16[64,6,3584]{2,1,0:T(8,128)(2,1)}, u32[]{:S(2)}, u32[]{:S(2)}) async-start(bf16[64,6,3584]{2,1,0:T(8,128)(2,1)} %all_to_all.49), calls=%async_computation.4 | async-start | bytes 7340032 | tf_op jit(solution)/shard_map/all_to_all | solution.py:102
  435.4 1.7 pad_maximum_fusion
  437.1 4.5 copy.35
  441.7 0.7 copy.31
  442.7 2.4 fusion.13
  445.2 3.4 fusion.1
  448.5 71.8 %all-to-all-done.4 = bf16[64,6,3584]{2,1,0:T(8,128)(2,1)} async-done(((bf16[64,6,3584]{2,1,0:T(8,128)(2,1)}), bf16[64,6,3584]{2,1,0:T(8,128)(2,1)}, u32[]{:S(2)}, u32[]{:S(2)}) %all-to-all-start.4) | async-done | bytes 2752544 | tf_op jit(solution)/shard_map/all_to_all | solution.py:102
  520.3 5.6 %all_to_all.51 = bf16[384,3584]{1,0:T(8,128)(2,1)} reshape(bf16[64,6,3584]{2,1,0:T(8,128)(2,1)} %all-to-all-done.4) | data formatting | bytes 5505024 | tf_op jit(solution)/shard_map/all_to_all | solution.py:102
  525.9 3.4 convolution_convert_fusion.4
  529.2 1.7 fusion.11
  (56 shorter events, 1.7 us)
Async XLA Ops:
  7.2 307.7 %copy-start = (bf16[128,3584]{1,0:T(8,128)(2,1)S(1)}, bf16[128,3584]{1,0:T(8,128)(2,1)}, u32[]{:S(2)}) copy-start(bf16[128,3584]{1,0:T(8,128)(2,1)} %param.8) | copy-start | bytes 2752516
  16.6 2.9 copy-start.8
  20.2 95.7 %copy-start.9 = (bf16[448,128]{1,0:T(8,128)(2,1)S(1)}, bf16[448,128]{1,0:T(8,128)(2,1)}, u32[]{:S(2)}) copy-start(bf16[448,128]{1,0:T(8,128)(2,1)} %param.12) | copy-start | bytes 344068
  115.9 11.4 %copy-start.10 = (bf16[448,128]{1,0:T(8,128)(2,1)S(1)}, bf16[448,128]{1,0:T(8,128)(2,1)}, u32[]{:S(2)}) copy-start(bf16[448,128]{1,0:T(8,128)(2,1)} %param.11) | copy-start | bytes 344068
  115.9 54.8 %copy-start.11 = (bf16[448,128]{1,0:T(8,128)(2,1)S(1)}, bf16[448,128]{1,0:T(8,128)(2,1)}, u32[]{:S(2)}) copy-start(bf16[448,128]{1,0:T(8,128)(2,1)} %param.13) | copy-start | bytes 344068
  116.9 90.2 %all-to-all-start.1 = ((bf16[8,448,128]{2,1,0:T(8,128)(2,1)}), bf16[8,448,128]{2,1,0:T(8,128)(2,1)S(1)}, u32[]{:S(2)}, u32[]{:S(2)}) async-start(bf16[8,448,128]{2,1,0:T(8,128)(2,1)} %tile.2), calls=%async_computation.1 | async-start | bytes 1835008 | tf_op jit(solution)/shard_map/all_to_all | solution.py:18
  207.2 3.0 copy-start.4
  207.2 3.0 copy-start.6
  218.1 6.4 %copy-start.12 = (f32[128,8]{0,1:T(8,128)S(1)}, f32[128,8]{0,1:T(8,128)}, u32[]{:S(2)}) copy-start(f32[128,8]{0,1:T(8,128)} %param.10) | copy-start | bytes 12292
  218.1 91.3 %all-to-all-start.2 = ((bf16[64,6,3584]{2,1,0:T(8,128)(2,1)}), bf16[64,6,3584]{2,1,0:T(8,128)(2,1)}, u32[]{:S(2)}, u32[]{:S(2)}) async-start(bf16[64,6,3584]{2,1,0:T(8,128)(2,1)} %all_to_all.43), calls=%async_computation.2 | async-start | bytes 7340032 | tf_op jit(solution)/shard_map/all_to_all | solution.py:69
  414.5 2.6 copy-start.3
  414.5 2.8 copy-start.7
  417.3 1.8 copy-start.2
  420.7 1.2 copy-start.5
  429.7 90.6 %all-to-all-start.4 = ((bf16[64,6,3584]{2,1,0:T(8,128)(2,1)}), bf16[64,6,3584]{2,1,0:T(8,128)(2,1)}, u32[]{:S(2)}, u32[]{:S(2)}) async-start(bf16[64,6,3584]{2,1,0:T(8,128)(2,1)} %all_to_all.49), calls=%async_computation.4 | async-start | bytes 7340032 | tf_op jit(solution)/shard_map/all_to_all | solution.py:102
  435.3 93.9 %reduce-scatter.4.cloned.1.call-start = ((), (), s32[]{:S(2)}) async-start(), calls=%async_computation.6 | async-start | bytes 3096576
  520.3 10.7 %copy-start.1 = (bf16[128,3584]{1,0:T(8,128)(2,1)S(1)}, bf16[128,3584]{1,0:T(8,128)(2,1)}, u32[]{:S(2)}) copy-start(bf16[128,3584]{1,0:T(8,128)(2,1)} %param.8) | copy-start | bytes 2752516
Sparse Core Ops, SparseCore 0:
  441.8 47.6 reduce-scatter.3
